TPU v7x, 512 devices: a whole 4x4x16 slice. The times are simulated.
512 devices in a mesh: gx: 32 (over y, x, core), vert: 16 (over z).
Axes of the slice: x: 4, y: 4, z: 16, core: 2. Of those that a mesh axis runs over, the one named last changes fastest.
Arguments:
- state: float32 [256, 16, 16384], P('gx', None, 'vert'), may hold values from -6 to 6
- macro: float32 [5, 256, 16], P(None, 'gx'), may hold values from -4 to 4
- relax_rate: float32 [256, 16], P('gx'), may hold values from 0.01 to 300, as said below
- velocity: float32 [3, 16384], P(None, 'vert'), may hold values from -2 to 4
- vel_sign: int32 [16384], P('vert'), may hold values from 0 to 1, as said below
- quad_weight: float32 [16384], P('vert'), may hold values from 0.5 to 2
- freestream: float32 [16, 16384], P(None, 'vert'), may hold values from -6 to 6
- wall_flag: int32 [16], replicated, may hold values 0 or 1
Outputs:
- new_state: float32 [256, 16, 16384], P('gx', None, 'vert')
- new_macro: float32 [5, 256, 16], P(None, 'gx')
Inputs may be any that keep to these rules, and one draw needn't show every extreme that they name: Each row of relax_rate varies from cell to cell. `vel_sign`: every aligned block of 1024 velocities holds both signs.
All inputs are finite; a program needn't handle non-finite values.
Results may differ from a plain program's by a relative error of at most 0.00013.
Values sent between devices are 32-bit elements; how exact they have to be, the bound alone decides.
No kernel may reach another device: no remote copies, remote signals or barrier semaphores. Data moves between devices by JAX's collectives and lax.ppermute only.
A program may use at most 64 MiB of HBM per device.

v0:
```python
import jax
import jax.numpy as jnp
from jax import lax
from jax.sharding import PartitionSpec as P

exact_mode = lax.Precision.HIGHEST


def prefix(value, axis, join, neutral, backward):
    count, mine = (lax.axis_size(axis), lax.axis_index(axis))
    pieces = jax.tree.map(lambda part: lax.all_gather(part, axis), value)
    if backward:
        pieces = jax.tree.map(lambda part: part[::-1], pieces)
        mine = count - 1 - mine
    total = jax.tree.map(
        lambda part, zero: jnp.full_like(part, 0) + jnp.asarray(zero, part.dtype), value, neutral
    )

    def turn(position, total):
        longer = join(total, jax.tree.map(lambda part: part[position], pieces))
        return jax.tree.map(lambda new, old: jnp.where(position < mine, new, old), longer, total)

    return lax.fori_loop(0, count - 1, turn, total)


def with_halo(cells, sides, width):
    for axis, dim in sides:
        count = lax.axis_size(axis)
        ends = count - 1
        head = lax.slice_in_dim(cells, 0, width, axis=dim)
        tail = lax.slice_in_dim(cells, cells.shape[dim] - width, cells.shape[dim], axis=dim)
        cells = jnp.concatenate(
            [
                lax.ppermute(tail, axis, [(i, (i + 1) % count) for i in range(ends)]),
                cells,
                lax.ppermute(head, axis, [((i + 1) % count, i) for i in range(ends)]),
            ],
            axis=dim,
        )
    return cells


def basis_sets(velocity, vel_sign, quad_weight, groups):
    magnitude = velocity[0]
    along_x = jnp.where(vel_sign == 1, magnitude, -magnitude)
    along_y = velocity[1]
    along_z = velocity[2]
    square = along_x * along_x + along_y * along_y + along_z * along_z
    ones_row = jnp.ones_like(along_x)
    equil_basis = jnp.stack([ones_row, 2.0 * along_x, 2.0 * along_y, 2.0 * along_z, square - 1.5])
    weights = quad_weight / (quad_weight.shape[0] * groups)
    heat_factor = 0.2 * (square - 2.5)
    moment_rows = jnp.stack(
        [
            ones_row,
            along_x,
            along_y,
            along_z,
            2.0 / 3.0 * square - 1.0,
            2.0 * along_x * along_y,
            2.0 * along_x * along_z,
            2.0 * along_y * along_z,
            2.0 * (along_x * along_x - square / 3.0),
            2.0 * (along_y * along_y - square / 3.0),
            heat_factor * along_x,
            heat_factor * along_y,
            heat_factor * along_z,
        ]
    )
    outflux = jnp.where(vel_sign == 0, weights * magnitude, 0.0)
    influx = jnp.where(vel_sign == 1, weights * magnitude, 0.0)
    return (magnitude, equil_basis, moment_rows * weights, outflux, influx)


def compose(earlier, latter):
    return (latter[0] * earlier[0], latter[0] * earlier[1] + latter[1])


def march_zero(decay, driven, reverse):

    def advance_cell(carried, pieces):
        zero_run = pieces[0] * carried[0] + pieces[1]
        product = pieces[0] * carried[1]
        return ((zero_run, product), (zero_run, product))

    initial = (jnp.zeros_like(driven[0]), jnp.ones_like(driven[0]))
    _, (zero_runs, products) = lax.scan(advance_cell, initial, (decay, driven), reverse=reverse)
    return (zero_runs, products)


def advance(padded, relax_cells):
    conserved = padded[:5]
    flow_x = jnp.stack(
        [
            padded[1],
            padded[0] + padded[4] + padded[8],
            padded[5],
            padded[6],
            2.0 / 3.0 * (padded[1] + padded[10]),
        ]
    )
    flow_y = jnp.stack(
        [
            padded[2],
            padded[5],
            padded[0] + padded[4] + padded[9],
            padded[7],
            2.0 / 3.0 * (padded[2] + padded[11]),
        ]
    )
    centre = conserved[:, 1:-1, 1:-1]
    laplace = (
        conserved[:, 2:, 1:-1]
        + conserved[:, :-2, 1:-1]
        + conserved[:, 1:-1, 2:]
        + conserved[:, 1:-1, :-2]
        - 4.0 * centre
    )
    divergence = (
        flow_x[:, 2:, 1:-1] - flow_x[:, :-2, 1:-1] + flow_y[:, 1:-1, 2:] - flow_y[:, 1:-1, :-2]
    )
    diffusivity = 0.2 / (1.0 + relax_cells)
    return (centre + diffusivity * laplace - 0.25 * divergence, centre)


def local(state, macro, relax_rate, velocity, vel_sign, quad_weight, freestream, wall_flag):
    cells_x = state.shape[0]
    cells_y = state.shape[1]
    vel_count = state.shape[2]
    slab_count = lax.axis_size("gx")
    slab_index = lax.axis_index("gx")
    magnitude, equil_basis, moment_basis, outflux, influx = basis_sets(
        velocity, vel_sign, quad_weight, lax.axis_size("vert")
    )
    courant = cells_x * slab_count * magnitude
    relax_cell = relax_rate[:, :, None]
    flat_macro = macro.reshape(macro.shape[0], cells_x * cells_y)
    equil_state = jnp.einsum("kc,kv->cv", flat_macro, equil_basis, precision=exact_mode).reshape(
        cells_x, cells_y, vel_count
    )
    source = state + relax_cell * equil_state
    wall_mask = wall_flag[:, None] == 1
    wall_in = jnp.sum(influx) / slab_count
    divisor = 1.0 + courant + relax_cell
    decay = courant / divisor
    driven = source / divisor
    back_runs, back_products = march_zero(decay, driven, True)
    fore_runs, fore_products = march_zero(decay, driven, False)
    ones_plane = jnp.ones((cells_y, vel_count), jnp.float32)
    zero_plane = jnp.zeros((cells_y, vel_count), jnp.float32)
    back_maps = prefix(
        (back_products[0], back_runs[0]), "gx", compose, (ones_plane, zero_plane), True
    )
    entry_back = back_maps[0] * freestream + back_maps[1]
    back = back_products * entry_back + back_runs
    at_anchor = slab_index == 0
    wall_out = jnp.where(at_anchor, jnp.dot(back[0], outflux, precision=exact_mode), 0.0)
    wall_out, wall_in = lax.psum((wall_out, wall_in), ("gx", "vert"))
    rho_wall = wall_out / wall_in
    inflow_left = jnp.where(wall_mask, rho_wall[:, None], freestream)
    fore_maps = prefix(
        (fore_products[-1], fore_runs[-1]), "gx", compose, (ones_plane, zero_plane), False
    )
    entry_fore = fore_maps[0] * inflow_left + fore_maps[1]
    fore = fore_products * entry_fore + fore_runs
    kinetic = jnp.where(vel_sign == 1, fore, back)
    flattened = kinetic.reshape(cells_x * cells_y, vel_count)
    partial_value = jnp.einsum("cv,kv->kc", flattened, moment_basis, precision=exact_mode).reshape(
        13, cells_x, cells_y
    )
    moments = lax.psum(partial_value, "vert")
    padded = with_halo(moments, (("gx", 1),), 1)
    padded = jnp.concatenate([padded[:, :, -1:], padded, padded[:, :, :1]], axis=2)
    updated, centre = advance(padded, relax_rate)
    change = updated - centre
    flat_change = change.reshape(change.shape[0], cells_x * cells_y)
    correction = jnp.einsum("kc,kv->cv", flat_change, equil_basis, precision=exact_mode).reshape(
        cells_x, cells_y, vel_count
    )
    return (kinetic + correction, updated)


def solution(mesh):
    return jax.shard_map(
        local,
        mesh=mesh,
        in_specs=(
            P("gx", None, "vert"),
            P(None, "gx", None),
            P("gx", None),
            P(None, "vert"),
            P("vert"),
            P("vert"),
            P(None, "vert"),
            P(),
        ),
        out_specs=(P("gx", None, "vert"), P(None, "gx", None)),
        check_vma=False,
    )
```

profile of v0, /device:TPU:7, one launch (start us, length us, event | category | flops | bytes accessed | tf_op | source)
XLA Modules:
  0.0 472.6 jit_solution(17301780224435400815)
XLA Ops:
  9.6 1.9 select_reduce_fusion
  12.1 1.2 add_divide_fusion
  19.7 58.5 %all-gather.9.cloned.1.call-done = f32[32,16,1024]{2,1,0:T(8,128)} async-done(((f32[1,16,1024]{2,1,0:T(8,128)}), f32[32,16,1024]{2,1,0:T(8,128)}) %all-gather.9.cloned.1.call-update) | async-done | bytes 2097168 | tf_op jit(solution)/shard_map/all_gather | solution.py:11
  78.2 1.7 rev.6
  79.9 59.8 %all-gather.11.cloned.1.call-done = f32[32,16,1024]{2,1,0:T(8,128)} async-done(((f32[1,16,1024]{2,1,0:T(8,128)}), f32[32,16,1024]{2,1,0:T(8,128)}) %all-gather.11.cloned.1.call-update) | async-done | bytes 2097168 | tf_op jit(solution)/shard_map/all_gather | solution.py:11
  139.6 3.2 rev.7
  142.9 28.3 %while.71 = (s32[]{:T(128)}, f32[16,1024]{1,0:T(8,128)S(1)}, f32[16,1024]{1,0:T(8,128)S(1)}, s32[]{:T(128)}, f32[32,16,1024]{2,1,0:T(8,128)S(1)}, /*index=5*/f32[32,16,1024]{2,1,0:T(8,128)}, s32[]{:T(128)}, s32[]{:T(128)}) while((s32[]{:T(128)}, f32[16,1024]{1,0:T(8,128)S(1)}, f32[16,1024]{1,0:T(8,128)S(1)}, s32[]{:T(128)}, ...), condition=%wide.region_7.8_spmd.clone, body=%wide.region_6.7_spmd.clone.sunk | while | flops 114692 | bytes 393325 | solution.py:23
  143.8 0.9 fusion.40
  144.7 0.9 fusion.40
  145.6 0.9 fusion.40
  146.5 0.9 fusion.40
  147.4 0.9 fusion.40
  148.4 0.9 fusion.40
  153.8 0.9 fusion.40
  154.7 0.9 fusion.40
  155.7 0.9 fusion.40
  159.3 0.9 fusion.40
  160.2 0.9 fusion.40
  162.1 0.9 fusion.40
  163.0 0.9 fusion.40
  163.9 0.9 fusion.40
  170.3 0.9 fusion.40
  171.2 0.9 multiply_add_fusion.2
  172.4 28.8 %all-gather.5.cloned.1.call-done = f32[32,16,1024]{2,1,0:T(8,128)} async-done(((f32[1,16,1024]{2,1,0:T(8,128)}), f32[32,16,1024]{2,1,0:T(8,128)}) %all-gather.5.cloned.1.call-update) | async-done | bytes 2097168 | tf_op jit(solution)/shard_map/all_gather | solution.py:11
  201.2 61.3 %all-gather.7.cloned.1.call-done = f32[32,16,1024]{2,1,0:T(8,128)} async-done(((f32[1,16,1024]{2,1,0:T(8,128)}), f32[32,16,1024]{2,1,0:T(8,128)}) %all-gather.7.cloned.1.call-update) | async-done | bytes 2097168 | tf_op jit(solution)/shard_map/all_gather | solution.py:11
  262.6 29.2 %while.70 = (s32[]{:T(128)}, f32[16,1024]{1,0:T(8,128)S(1)}, f32[16,1024]{1,0:T(8,128)S(1)}, s32[]{:T(128)}, f32[32,16,1024]{2,1,0:T(8,128)}, /*index=5*/f32[32,16,1024]{2,1,0:T(8,128)}, s32[]{:T(128)}, s32[]{:T(128)}) while((s32[]{:T(128)}, f32[16,1024]{1,0:T(8,128)S(1)}, f32[16,1024]{1,0:T(8,128)S(1)}, s32[]{:T(128)}, ...), condition=%wide.region_3.4_spmd.clone, body=%wide.region_2.3_spmd.clone.sunk | while | flops 114692 | bytes 393325 | solution.py:23
  262.6 0.9 fusion.39
  263.5 0.9 fusion.39
  264.4 0.9 fusion.39
  265.4 0.9 fusion.39
  266.3 0.9 fusion.39
  267.3 0.9 fusion.39
  268.2 0.9 fusion.39
  269.2 0.9 fusion.39
  270.1 0.9 fusion.39
  271.1 0.9 fusion.39
  272.0 0.9 fusion.39
  272.9 0.9 fusion.39
  273.9 0.9 fusion.39
  274.8 0.9 fusion.39
  275.8 0.9 fusion.39
  276.7 0.9 fusion.39
  277.7 0.9 fusion.39
  278.6 0.9 fusion.39
  279.6 0.9 fusion.39
  280.5 0.9 fusion.39
  281.4 0.9 fusion.39
  282.4 0.9 fusion.39
  283.3 0.9 fusion.39
  284.3 0.9 fusion.39
  285.2 0.9 fusion.39
  286.2 0.9 fusion.39
  287.1 0.9 fusion.39
  288.0 0.9 fusion.39
  289.0 0.9 fusion.39
  289.9 0.9 fusion.39
  290.9 0.9 fusion.39
  291.8 103.7 %all-reduce = (f32[16]{0:T(128)S(1)}, f32[]{:T(128)}) all-reduce(f32[16]{0:T(128)S(1)} %fusion.2, f32[]{:T(128)S(6)} %div.41), channel_id=1, replica_groups=mesh['gx'=32,'vert'=16] {'gx','vert'}, use_global_device_ids=true, to_apply=%region_8.9 | all-reduce | flops 17 | bytes 136 | tf_op jit(solution)/shard_map/psum | solution.py:158
  396.4 1.9 fusion.3
  398.4 40.2 %psum.23 = f32[13,8,16]{2,0,1:T(8,128)S(1)} all-reduce(f32[13,8,16]{2,0,1:T(8,128)S(1)} %fusion.3), channel_id=1, replica_groups=mesh['gx'=32,'vert'=16] {'vert'}, use_global_device_ids=true, to_apply=%region_11.12 | all-reduce | flops 1664 | bytes 13312 | tf_op jit(solution)/shard_map/psum | solution.py:171
  438.6 17.3 %collective-permute-start.1 = (f32[13,1,16]{2,0,1:T(8,128)S(1)}, f32[13,1,16]{2,0,1:T(8,128)S(1)}, u32[]{:S(2)}, u32[]{:S(2)}) collective-permute-start(f32[13,1,16]{2,0,1:T(8,128)S(1)} %get-tuple-element.544), channel_id=1, source_target_pairs={{0,16},{16,32},{32,48},{48,64},{64,80},{80,96},{96,112},{112,128},... | collective-permute-start | bytes 2504 | tf_op jit(solution)/shard_map/ppermute | solution.py:34
  455.9 1.9 collective-permute-start
  457.9 5.1 %collective-permute-done = f32[13,1,16]{2,0,1:T(8,128)S(1)} collective-permute-done((f32[13,1,16]{2,0,1:T(8,128)S(1)}, f32[13,1,16]{2,0,1:T(8,128)S(1)}, u32[]{:S(2)}, u32[]{:S(2)}) %collective-permute-start) | collective-permute-done | bytes 864 | tf_op jit(solution)/shard_map/ppermute | solution.py:36
  464.0 1.5 convolution_add_fusion
  (111 shorter events, 26.1 us)
Async XLA Ops:
  7.2 71.0 %all-gather.9.cloned.1.call-start = ((), (), s32[]{:S(2)}) async-start(), calls=%async_computation.2 | async-start | bytes 2162688 | tf_op jit(solution)/shard_map/all_gather | solution.py:11
  9.6 4.0 copy-start.7
  14.7 125.0 %all-gather.11.cloned.1.call-start = ((), (), s32[]{:S(2)}) async-start(), calls=%async_computation.3 | async-start | bytes 2162688 | tf_op jit(solution)/shard_map/all_gather | solution.py:11
  15.4 185.8 %all-gather.5.cloned.1.call-start = ((), (), s32[]{:S(2)}) async-start(), calls=%async_computation | async-start | bytes 2162688 | tf_op jit(solution)/shard_map/all_gather | solution.py:11
  15.5 2.1 copy-start.5
  15.5 2.2 copy-start.10
  16.2 3.5 copy-start
  16.2 3.5 copy-start.2
  16.9 245.7 %all-gather.7.cloned.1.call-start = ((), (), s32[]{:S(2)}) async-start(), calls=%async_computation.1 | async-start | bytes 2162688 | tf_op jit(solution)/shard_map/all_gather | solution.py:11
  171.2 225.0 %copy-start.4 = (f32[16,1024]{1,0:T(8,128)S(1)}, f32[16,1024]{1,0:T(8,128)}, u32[]{:S(2)}) copy-start(f32[16,1024]{1,0:T(8,128)} %param.22) | copy-start | bytes 196612
  171.2 225.0 %copy-start.9 = (pred[16]{0:T(512)(128)(4,1)S(1)}, pred[16]{0:T(512)(128)(4,1)}, u32[]{:S(2)}) copy-start(pred[16]{0:T(512)(128)(4,1)} %broadcast_compare_fusion.1) | copy-start | bytes 52
  172.1 224.2 %copy-start.1 = (f32[8,16,1024]{2,1,0:T(8,128)S(1)}, f32[8,16,1024]{2,1,0:T(8,128)}, u32[]{:S(2)}) copy-start(f32[8,16,1024]{2,1,0:T(8,128)} %copy-done) | copy-start | bytes 1572868
  172.1 224.2 %copy-start.3 = (f32[8,16,1024]{2,1,0:T(8,128)S(1)}, f32[8,16,1024]{2,1,0:T(8,128)}, u32[]{:S(2)}) copy-start(f32[8,16,1024]{2,1,0:T(8,128)} %copy-done.2) | copy-start | bytes 1572868
  172.1 224.2 %copy-start.8 = (pred[1024]{0:T(1024)(128)(4,1)S(1)}, pred[1024]{0:T(1024)(128)(4,1)}, u32[]{:S(2)}) copy-start(pred[1024]{0:T(1024)(128)(4,1)} %copy-done.7) | copy-start | bytes 3076
  291.8 164.1 %copy-start.6 = (f32[8,16]{1,0:T(8,128)S(1)}, f32[8,16]{1,0:T(8,128)}, u32[]{:S(2)}) copy-start(f32[8,16]{1,0:T(8,128)} %param.18) | copy-start | bytes 1540
  438.6 19.3 %collective-permute-start.1 = (f32[13,1,16]{2,0,1:T(8,128)S(1)}, f32[13,1,16]{2,0,1:T(8,128)S(1)}, u32[]{:S(2)}, u32[]{:S(2)}) collective-permute-start(f32[13,1,16]{2,0,1:T(8,128)S(1)} %get-tuple-element.544), channel_id=1, source_target_pairs={{0,16},{16,32},{32,48},{48,64},{64,80},{80,96},{96,112},{112,128},... | collective-permute-start | bytes 2504 | tf_op jit(solution)/shard_map/ppermute | solution.py:34
  455.9 7.1 %collective-permute-start = (f32[13,1,16]{2,0,1:T(8,128)S(1)}, f32[13,1,16]{2,0,1:T(8,128)S(1)}, u32[]{:S(2)}, u32[]{:S(2)}) collective-permute-start(f32[13,1,16]{2,0,1:T(8,128)S(1)} %get-tuple-element.543), channel_id=1, source_target_pairs={{16,0},{32,16},{48,32},{64,48},{80,64},{96,80},{112,96},{128,112},... | collective-permute-start | bytes 2504 | tf_op jit(solution)/shard_map/ppermute | solution.py:36
Sparse Core Ops, SparseCore 0:
  14.8 63.3 all-gather.8
  81.3 58.3 all-gather.10
  142.8 58.3 all-gather.4
  204.2 58.3 all-gather.6
where the time goes:
time: 476 us; the launch traced here: 473 us
  waiting for transfers between devices  214 us (45%)
  blocking collectives  144 us (30%)
  other arithmetic  64.6 us (14%)
  starting transfers between devices  19.4 us (4%)
  between operations  14.8 us (3%)
  local copies, waits for them, and re-layouts  10.4 us (2%)
    all_gather x4, waiting for transfers between devices, prefix(): pieces = jax.tree.map(lambda part: lax.all_gather(part, axis), value)  208 us
    psum x1, blocking collectives, local(): wall_out, wall_in = lax.psum((wall_out, wall_in), ('gx', 'vert'))  104 us
    select_n x62, other arithmetic, turn(): jnp.where(position < mine, new, old)  56.1 us
    psum x1, blocking collectives, local(): moments = lax.psum(partial_value, 'vert')  40.2 us
    ppermute x1, starting transfers between devices, with_halo(): lax.ppermute(tail, axis, [(i, (i + 1) % count) for i in range(ends)])  17.3 us
  transfers between devices with their start and end apart: 6, of which 5 were waited for; matrix products, arithmetic and copies ran while one was open for 8% of the time, Pallas kernels for 0%

commit v1 on v0

--- a/solution.py
+++ b/solution.py
@@ -168,7 +168,13 @@
     partial_value = jnp.einsum("cv,kv->kc", flattened, moment_basis, precision=exact_mode).reshape(
         13, cells_x, cells_y
     )
-    moments = lax.psum(partial_value, "vert")
+    size = lax.axis_size("vert")
+    moments, reach = (partial_value, 1)
+    while reach < size:
+        moments = moments + lax.ppermute(
+            moments, "vert", [(i_2, i_2 ^ reach) for i_2 in range(size)]
+        )
+        reach = 2 * reach
     padded = with_halo(moments, (("gx", 1),), 1)
     padded = jnp.concatenate([padded[:, :, -1:], padded, padded[:, :, :1]], axis=2)
     updated, centre = advance(padded, relax_rate)

time: 476 us -> 461 us (0.968)
  blocking collectives: 144 us -> 104 us
  waiting for transfers between devices: 214 us -> 228 us
  starting transfers between devices: 19.4 us -> 27 us
    psum x1 -> x0, blocking collectives: 40.2 us -> none  [local(): moments = lax.psum(partial_value, 'vert')]
    ppermute x0 -> x4, waiting for transfers between devices: none -> 18.6 us  [local(): lax.ppermute(moments, 'vert', [(i_2, i_2 ^ reach) for i_2 in range(size)])]
    ppermute x0 -> x4, starting transfers between devices: none -> 16.8 us  [local(): lax.ppermute(moments, 'vert', [(i_2, i_2 ^ reach) for i_2 in range(size)])]
    ppermute x1, starting transfers between devices: 17.3 us -> 3 us  [with_halo(): lax.ppermute(tail, axis, [(i, (i + 1) % count) for i in range(ends)])]
    ppermute x1, starting transfers between devices: 1.92 us -> 7.05 us  [with_halo(): lax.ppermute(head, axis, [((i + 1) % count, i) for i in range(ends)])]
    ppermute x1, waiting for transfers between devices: 5.12 us -> 0.01 us  [with_halo(): lax.ppermute(head, axis, [((i + 1) % count, i) for i in range(ends)])]
  transfers between devices with their start and end apart: 6 -> 10, of which waited for: 5 -> 9; matrix products, arithmetic and copies ran while one was open for 8% -> 8% of each run, Pallas kernels for 0% -> 0%
where the time goes in v1:
time: 461 us; the launch traced here: 454 us
  waiting for transfers between devices  228 us (49%)
  blocking collectives  104 us (23%)
  other arithmetic  64.7 us (14%)
  starting transfers between devices  27 us (6%)
  between operations  14.9 us (3%)
  local copies, waits for them, and re-layouts  10.4 us (2%)
    all_gather x4, waiting for transfers between devices, prefix(): pieces = jax.tree.map(lambda part: lax.all_gather(part, axis), value)  208 us
    psum x1, blocking collectives, local(): wall_out, wall_in = lax.psum((wall_out, wall_in), ('gx', 'vert'))  104 us
    select_n x62, other arithmetic, turn(): jnp.where(position < mine, new, old)  56.1 us
    ppermute x4, waiting for transfers between devices, local(): lax.ppermute(moments, 'vert', [(i_2, i_2 ^ reach) for i_2 in range(size)])  18.6 us
    ppermute x4, starting transfers between devices, local(): lax.ppermute(moments, 'vert', [(i_2, i_2 ^ reach) for i_2 in range(size)])  16.8 us
  transfers between devices with their start and end apart: 10, of which 9 were waited for; matrix products, arithmetic and copies ran while one was open for 8% of the time, Pallas kernels for 0%

profile of v1, /device:TPU:7, one launch (start us, length us, event | category | flops | bytes accessed | tf_op | source)
XLA Modules:
  0.0 454.5 jit_solution(2442360994557481985)
XLA Ops:
  9.6 1.9 select_reduce_fusion
  12.2 1.2 add_divide_fusion
  19.6 58.5 %all-gather.9.cloned.1.call-done = f32[32,16,1024]{2,1,0:T(8,128)} async-done(((f32[1,16,1024]{2,1,0:T(8,128)}), f32[32,16,1024]{2,1,0:T(8,128)}) %all-gather.9.cloned.1.call-update) | async-done | bytes 2097168 | tf_op jit(solution)/shard_map/all_gather | solution.py:11
  78.2 1.7 rev.6
  79.9 59.8 %all-gather.11.cloned.1.call-done = f32[32,16,1024]{2,1,0:T(8,128)} async-done(((f32[1,16,1024]{2,1,0:T(8,128)}), f32[32,16,1024]{2,1,0:T(8,128)}) %all-gather.11.cloned.1.call-update) | async-done | bytes 2097168 | tf_op jit(solution)/shard_map/all_gather | solution.py:11
  139.7 3.2 rev.7
  142.9 28.3 %while.71 = (s32[]{:T(128)}, f32[16,1024]{1,0:T(8,128)S(1)}, f32[16,1024]{1,0:T(8,128)S(1)}, s32[]{:T(128)}, f32[32,16,1024]{2,1,0:T(8,128)S(1)}, /*index=5*/f32[32,16,1024]{2,1,0:T(8,128)}, s32[]{:T(128)}, s32[]{:T(128)}) while((s32[]{:T(128)}, f32[16,1024]{1,0:T(8,128)S(1)}, f32[16,1024]{1,0:T(8,128)S(1)}, s32[]{:T(128)}, ...), condition=%wide.region_7.8_spmd.clone, body=%wide.region_6.7_spmd.clone.sunk | while | flops 114692 | bytes 393325 | solution.py:23
  149.3 0.9 fusion.40
  150.2 0.9 fusion.40
  151.1 0.9 fusion.40
  152.0 0.9 fusion.40
  158.4 0.9 fusion.40
  159.3 0.9 fusion.40
  160.2 0.9 fusion.40
  162.1 0.9 fusion.40
  168.5 0.9 fusion.40
  171.2 0.9 multiply_add_fusion.2
  172.4 28.8 %all-gather.5.cloned.1.call-done = f32[32,16,1024]{2,1,0:T(8,128)} async-done(((f32[1,16,1024]{2,1,0:T(8,128)}), f32[32,16,1024]{2,1,0:T(8,128)}) %all-gather.5.cloned.1.call-update) | async-done | bytes 2097168 | tf_op jit(solution)/shard_map/all_gather | solution.py:11
  201.2 61.3 %all-gather.7.cloned.1.call-done = f32[32,16,1024]{2,1,0:T(8,128)} async-done(((f32[1,16,1024]{2,1,0:T(8,128)}), f32[32,16,1024]{2,1,0:T(8,128)}) %all-gather.7.cloned.1.call-update) | async-done | bytes 2097168 | tf_op jit(solution)/shard_map/all_gather | solution.py:11
  262.5 29.2 %while.70 = (s32[]{:T(128)}, f32[16,1024]{1,0:T(8,128)S(1)}, f32[16,1024]{1,0:T(8,128)S(1)}, s32[]{:T(128)}, f32[32,16,1024]{2,1,0:T(8,128)}, /*index=5*/f32[32,16,1024]{2,1,0:T(8,128)}, s32[]{:T(128)}, s32[]{:T(128)}) while((s32[]{:T(128)}, f32[16,1024]{1,0:T(8,128)S(1)}, f32[16,1024]{1,0:T(8,128)S(1)}, s32[]{:T(128)}, ...), condition=%wide.region_3.4_spmd.clone, body=%wide.region_2.3_spmd.clone.sunk | while | flops 114692 | bytes 393325 | solution.py:23
  262.5 0.9 fusion.39
  263.4 0.9 fusion.39
  264.4 0.9 fusion.39
  265.3 0.9 fusion.39
  266.3 0.9 fusion.39
  267.2 0.9 fusion.39
  268.2 0.9 fusion.39
  269.1 0.9 fusion.39
  270.0 0.9 fusion.39
  271.0 0.9 fusion.39
  271.9 0.9 fusion.39
  272.9 0.9 fusion.39
  273.8 0.9 fusion.39
  274.8 0.9 fusion.39
  275.7 0.9 fusion.39
  276.7 0.9 fusion.39
  277.6 0.9 fusion.39
  278.5 0.9 fusion.39
  279.5 0.9 fusion.39
  280.4 0.9 fusion.39
  281.4 0.9 fusion.39
  282.3 0.9 fusion.39
  283.3 0.9 fusion.39
  284.2 0.9 fusion.39
  285.2 0.9 fusion.39
  286.1 0.9 fusion.39
  287.0 0.9 fusion.39
  288.0 0.9 fusion.39
  288.9 0.9 fusion.39
  289.9 0.9 fusion.39
  290.8 0.9 fusion.39
  291.8 103.7 %all-reduce = (f32[16]{0:T(128)S(1)}, f32[]{:T(128)}) all-reduce(f32[16]{0:T(128)S(1)} %fusion.2, f32[]{:T(128)S(6)} %div.41), channel_id=1, replica_groups=mesh['gx'=32,'vert'=16] {'gx','vert'}, use_global_device_ids=true, to_apply=%region_8.9 | all-reduce | flops 17 | bytes 136 | tf_op jit(solution)/shard_map/psum | solution.py:158
  396.4 1.9 fusion.3
  398.3 1.9 collective-permute-start
  400.2 3.1 collective-permute-done
  403.3 2.3 collective-permute-start.1
  405.6 4.1 collective-permute-done.1
  409.7 4.0 collective-permute-start.2
  413.7 6.4 %collective-permute-done.2 = f32[13,8,16]{2,0,1:T(8,128)S(1)} collective-permute-done((f32[13,8,16]{2,0,1:T(8,128)S(1)}, f32[13,8,16]{2,0,1:T(8,128)S(1)}, u32[]{:S(2)}, u32[]{:S(2)}) %collective-permute-start.2) | collective-permute-done | bytes 6688 | tf_op jit(solution)/shard_map/ppermute | solution.py:174
  420.1 8.6 %collective-permute-start.3 = (f32[13,8,16]{2,0,1:T(8,128)S(1)}, f32[13,8,16]{2,0,1:T(8,128)S(1)}, u32[]{:S(2)}, u32[]{:S(2)}) collective-permute-start(f32[13,8,16]{2,0,1:T(8,128)S(1)} %add.208), channel_id=1, source_target_pairs={{0,8},{1,9},{2,10},{3,11},{4,12},{5,13},{6,14},{7,15},{8,0},{9,1},... | collective-permute-start | bytes 19976 | tf_op jit(solution)/shard_map/ppermute | solution.py:174
  428.7 5.1 %collective-permute-done.3 = f32[13,8,16]{2,0,1:T(8,128)S(1)} collective-permute-done((f32[13,8,16]{2,0,1:T(8,128)S(1)}, f32[13,8,16]{2,0,1:T(8,128)S(1)}, u32[]{:S(2)}, u32[]{:S(2)}) %collective-permute-start.3) | collective-permute-done | bytes 6688 | tf_op jit(solution)/shard_map/ppermute | solution.py:174
  433.8 7.1 %collective-permute-start.4 = (f32[13,1,16]{2,0,1:T(8,128)S(1)}, f32[13,1,16]{2,0,1:T(8,128)S(1)}, u32[]{:S(2)}, u32[]{:S(2)}) collective-permute-start(f32[13,1,16]{2,0,1:T(8,128)S(1)} %get-tuple-element.543), channel_id=1, source_target_pairs={{16,0},{32,16},{48,32},{64,48},{80,64},{96,80},{112,96},{128,112},... | collective-permute-start | bytes 2504 | tf_op jit(solution)/shard_map/ppermute | solution.py:36
  440.9 3.0 collective-permute-start.5
  445.9 1.5 convolution_add_fusion
  (122 shorter events, 32.3 us)
Async XLA Ops:
  7.2 71.0 %all-gather.9.cloned.1.call-start = ((), (), s32[]{:S(2)}) async-start(), calls=%async_computation.2 | async-start | bytes 2162688 | tf_op jit(solution)/shard_map/all_gather | solution.py:11
  9.6 4.0 copy-start.7
  14.7 125.0 %all-gather.11.cloned.1.call-start = ((), (), s32[]{:S(2)}) async-start(), calls=%async_computation.3 | async-start | bytes 2162688 | tf_op jit(solution)/shard_map/all_gather | solution.py:11
  15.4 185.7 %all-gather.5.cloned.1.call-start = ((), (), s32[]{:S(2)}) async-start(), calls=%async_computation | async-start | bytes 2162688 | tf_op jit(solution)/shard_map/all_gather | solution.py:11
  15.5 2.2 copy-start.5
  15.5 2.2 copy-start.10
  16.2 3.5 copy-start
  16.2 3.5 copy-start.2
  16.9 245.6 %all-gather.7.cloned.1.call-start = ((), (), s32[]{:S(2)}) async-start(), calls=%async_computation.1 | async-start | bytes 2162688 | tf_op jit(solution)/shard_map/all_gather | solution.py:11
  171.2 224.9 %copy-start.4 = (f32[16,1024]{1,0:T(8,128)S(1)}, f32[16,1024]{1,0:T(8,128)}, u32[]{:S(2)}) copy-start(f32[16,1024]{1,0:T(8,128)} %param.22) | copy-start | bytes 196612
  171.2 224.9 %copy-start.9 = (pred[16]{0:T(512)(128)(4,1)S(1)}, pred[16]{0:T(512)(128)(4,1)}, u32[]{:S(2)}) copy-start(pred[16]{0:T(512)(128)(4,1)} %broadcast_compare_fusion.1) | copy-start | bytes 52
  172.1 224.1 %copy-start.1 = (f32[8,16,1024]{2,1,0:T(8,128)S(1)}, f32[8,16,1024]{2,1,0:T(8,128)}, u32[]{:S(2)}) copy-start(f32[8,16,1024]{2,1,0:T(8,128)} %copy-done) | copy-start | bytes 1572868
  172.1 224.1 %copy-start.3 = (f32[8,16,1024]{2,1,0:T(8,128)S(1)}, f32[8,16,1024]{2,1,0:T(8,128)}, u32[]{:S(2)}) copy-start(f32[8,16,1024]{2,1,0:T(8,128)} %copy-done.2) | copy-start | bytes 1572868
  172.2 224.1 %copy-start.8 = (pred[1024]{0:T(1024)(128)(4,1)S(1)}, pred[1024]{0:T(1024)(128)(4,1)}, u32[]{:S(2)}) copy-start(pred[1024]{0:T(1024)(128)(4,1)} %copy-done.7) | copy-start | bytes 3076
  291.8 152.1 %copy-start.6 = (f32[8,16]{1,0:T(8,128)S(1)}, f32[8,16]{1,0:T(8,128)}, u32[]{:S(2)}) copy-start(f32[8,16]{1,0:T(8,128)} %param.18) | copy-start | bytes 1540
  398.3 5.0 %collective-permute-start = (f32[13,8,16]{2,0,1:T(8,128)S(1)}, f32[13,8,16]{2,0,1:T(8,128)S(1)}, u32[]{:S(2)}, u32[]{:S(2)}) collective-permute-start(f32[13,8,16]{2,0,1:T(8,128)S(1)} %fusion.3), channel_id=1, source_target_pairs={{0,1},{1,0},{2,3},{3,2},{4,5},{5,4},{6,7},{7,6},{8,9},{9,8},{10,11... | collective-permute-start | bytes 19976 | tf_op jit(solution)/shard_map/ppermute | solution.py:174
  403.3 6.3 %collective-permute-start.1 = (f32[13,8,16]{2,0,1:T(8,128)S(1)}, f32[13,8,16]{2,0,1:T(8,128)S(1)}, u32[]{:S(2)}, u32[]{:S(2)}) collective-permute-start(f32[13,8,16]{2,0,1:T(8,128)S(1)} %add.206), channel_id=1, source_target_pairs={{0,2},{1,3},{2,0},{3,1},{4,6},{5,7},{6,4},{7,5},{8,10},{9,11},{10,... | collective-permute-start | bytes 19976 | tf_op jit(solution)/shard_map/ppermute | solution.py:174
  409.7 10.4 %collective-permute-start.2 = (f32[13,8,16]{2,0,1:T(8,128)S(1)}, f32[13,8,16]{2,0,1:T(8,128)S(1)}, u32[]{:S(2)}, u32[]{:S(2)}) collective-permute-start(f32[13,8,16]{2,0,1:T(8,128)S(1)} %add.207), channel_id=1, source_target_pairs={{0,4},{1,5},{2,6},{3,7},{4,0},{5,1},{6,2},{7,3},{8,12},{9,13},{10,... | collective-permute-start | bytes 19976 | tf_op jit(solution)/shard_map/ppermute | solution.py:174
  420.1 13.7 %collective-permute-start.3 = (f32[13,8,16]{2,0,1:T(8,128)S(1)}, f32[13,8,16]{2,0,1:T(8,128)S(1)}, u32[]{:S(2)}, u32[]{:S(2)}) collective-permute-start(f32[13,8,16]{2,0,1:T(8,128)S(1)} %add.208), channel_id=1, source_target_pairs={{0,8},{1,9},{2,10},{3,11},{4,12},{5,13},{6,14},{7,15},{8,0},{9,1},... | collective-permute-start | bytes 19976 | tf_op jit(solution)/shard_map/ppermute | solution.py:174
  433.8 10.1 %collective-permute-start.4 = (f32[13,1,16]{2,0,1:T(8,128)S(1)}, f32[13,1,16]{2,0,1:T(8,128)S(1)}, u32[]{:S(2)}, u32[]{:S(2)}) collective-permute-start(f32[13,1,16]{2,0,1:T(8,128)S(1)} %get-tuple-element.543), channel_id=1, source_target_pairs={{16,0},{32,16},{48,32},{64,48},{80,64},{96,80},{112,96},{128,112},... | collective-permute-start | bytes 2504 | tf_op jit(solution)/shard_map/ppermute | solution.py:36
  440.9 3.8 collective-permute-start.5
Sparse Core Ops, SparseCore 0:
  14.8 63.3 all-gather.8
  81.3 58.3 all-gather.10
  142.8 58.3 all-gather.4
  204.1 58.3 all-gather.6
